TPU v7x, 256 devices: a whole 4x4x8 slice. The times are simulated.
256 devices in a mesh: row: 32 (over y, z), col: 8 (over x, core).
Axes of the slice: x: 4, y: 4, z: 8, core: 2. Of those that a mesh axis runs over, the one named last changes fastest.
Arguments:
- tokens: bfloat16 [1536, 8192], P('row', 'col'), may hold values from -6 to 6
- weight: bfloat16 [8192, 32768], P('col', 'row'), may hold values from -0.109375 to 0.109375
- tile_rows: int32 [32, 8, 32], P('row', 'col'), may hold values from 0 to 63, as said below
- tile_cols: int32 [32, 8, 32], P('row', 'col'), may hold values from 0 to 255, as said below
- tile_count: int32 [32, 8], P('row', 'col'), may hold values from 8 to 32, as said below
- hidden_cotangent: bfloat16 [1536, 32768], P('col', 'row'), may hold values from -6 to 6
Outputs:
- hidden: bfloat16 [1536, 32768], P('col', 'row')
- input_grad: bfloat16 [1536, 8192], P('row', 'col')
- weight_grad: bfloat16 [8192, 32768], P('col', 'row')
Inputs may be any that keep to these rules, and one draw needn't show every extreme that they name: tile_rows[r, c, k] is a row block of the weight (tiles of 128 x 128) among the 8 blocks from c * 8 on, which index c of col holds. tile_cols[r, c, k] is a column block among the 8 blocks from r * 8 on, which index r of row holds; the 32 candidate tiles of one device are distinct. The first tile_count[r, c] candidates of device (r, c) are its nonzero tiles; some device holds 32.
All inputs are finite; a program needn't handle non-finite values.
Results may differ from a plain program's by a relative error of at most 0.0049.
Values may be sent and summed in bfloat16 or wider, within the bound.
No kernel may reach another device: no remote copies, remote signals or barrier semaphores. Data moves between devices by JAX's collectives and lax.ppermute only.
A program may use at most 128 MiB of HBM per device.

v0:
```python
import jax
import jax.numpy as jnp
from jax import lax
from jax.sharding import Mesh
from jax.sharding import PartitionSpec as P

TILE = 128
ROW = ("row_0", "row_1")


def laid_out(pieces, dim):
    pieces = jnp.moveaxis(pieces, 0, dim)
    dims = pieces.shape
    return pieces.reshape(*dims[:dim], dims[dim] * dims[dim + 1], *dims[dim + 2 :])


def all_blocks(shard, axes, turns):
    pieces = shard
    for k in turns:
        pieces = lax.all_gather(pieces, axes[k])
    done = turns[::-1]
    back = [done.index(k) for k in range(len(axes))]
    pieces = pieces.transpose(*back, *range(len(axes), pieces.ndim))
    return pieces.reshape(-1, *shard.shape)


def gathered_by_axis(shard, axes, turns, dim):
    return laid_out(all_blocks(shard, axes, turns), dim)


def own_rows(so_far, axes):
    for axis in axes:
        so_far = lax.psum_scatter(so_far, axis, scatter_dimension=0, tiled=True)
    return so_far


def sparse_apply(inputs, live_tiles, in_index, out_index, out_blocks, flipped):
    count_rows, in_width = inputs.shape
    in_blocks = in_width // TILE
    block_rows = 128
    picker = (in_index[:, None] == jnp.arange(in_blocks)[None, :]).astype(jnp.bfloat16)
    placer = (out_index[:, None] == jnp.arange(out_blocks)[None, :]).astype(jnp.float32)

    def per_block(rows_block):
        shaped_rows = rows_block.reshape(block_rows, in_blocks, TILE)
        pieces = jnp.einsum(
            "bjp,kj->bkp", shaped_rows, picker, preferred_element_type=jnp.float32
        ).astype(jnp.bfloat16)
        if flipped:
            product = jnp.einsum(
                "bkq,kpq->bkp", pieces, live_tiles, preferred_element_type=jnp.float32
            )
        else:
            product = jnp.einsum(
                "bkp,kpq->bkq", pieces, live_tiles, preferred_element_type=jnp.float32
            )
        placed = jnp.einsum("bkq,kc->bcq", product, placer, precision=lax.Precision.HIGHEST)
        return placed.reshape(block_rows, out_blocks * TILE)

    stacked = inputs.reshape(count_rows // block_rows, block_rows, in_width)
    return lax.map(per_block, stacked).reshape(count_rows, out_blocks * TILE)


def tile_grads(full_tokens, full_grads, local_rows, local_cols, is_live, row_blocks, col_blocks):
    count_rows = full_tokens.shape[0]
    block_rows = 128
    steps_count = count_rows // block_rows
    left_side = full_tokens.reshape(steps_count, block_rows, row_blocks, TILE)
    right_side = full_grads.reshape(steps_count, block_rows, col_blocks, TILE)

    def accumulate(running, block_pair):
        token_block, grad_block = block_pair
        product = jnp.einsum(
            "bkp,bkq->kpq",
            token_block[:, local_rows],
            grad_block[:, local_cols],
            preferred_element_type=jnp.float32,
        )
        return (running + product, None)

    start_sums = jnp.zeros((local_rows.shape[0], TILE, TILE), jnp.float32)
    tile_sums, leftover = lax.scan(accumulate, start_sums, (left_side, right_side))
    tile_sums = tile_sums * is_live[:, None, None].astype(jnp.float32)
    slot_ids = local_rows * col_blocks + local_cols
    placed = (
        jnp.zeros((row_blocks * col_blocks, TILE, TILE), jnp.float32).at[slot_ids].add(tile_sums)
    )
    placed = placed.reshape(row_blocks, col_blocks, TILE, TILE).transpose(0, 2, 1, 3)
    return placed.reshape(row_blocks * TILE, col_blocks * TILE).astype(jnp.bfloat16)


def on_device(tokens, weight, tile_rows, tile_cols, tile_count, hidden_cotangent):
    row_index = lax.axis_index(ROW)
    col_index = lax.axis_index("col")
    row_blocks = weight.shape[0] // TILE
    col_blocks = weight.shape[1] // TILE
    capacity = tile_rows.shape[2]
    local_rows = tile_rows.reshape(capacity) - col_index * row_blocks
    local_cols = tile_cols.reshape(capacity) - row_index * col_blocks
    is_live = jnp.arange(capacity) < tile_count.reshape(())
    shaped = weight.reshape(row_blocks, TILE, col_blocks, TILE)
    live_tiles = shaped[local_rows, :, local_cols, :] * is_live[:, None, None].astype(jnp.bfloat16)
    full_tokens = gathered_by_axis(tokens, ROW, (0, 1), 0)
    pre_act = lax.psum_scatter(
        sparse_apply(full_tokens, live_tiles, local_rows, local_cols, col_blocks, False),
        "col",
        scatter_dimension=0,
        tiled=True,
    )
    gate_value = jax.nn.sigmoid(pre_act)
    hidden = (pre_act * gate_value).astype(jnp.bfloat16)
    silu_slope = gate_value * (1.0 + pre_act * (1.0 - gate_value))
    grad_pre = (hidden_cotangent.astype(jnp.float32) * silu_slope).astype(jnp.bfloat16)
    full_grads = lax.all_gather(grad_pre, "col", axis=0, tiled=True)
    input_grad = own_rows(
        sparse_apply(full_grads, live_tiles, local_cols, local_rows, row_blocks, True), ROW
    ).astype(jnp.bfloat16)
    weight_grad = tile_grads(
        full_tokens, full_grads, local_rows, local_cols, is_live, row_blocks, col_blocks
    )
    return (hidden, input_grad, weight_grad)


def solution(mesh):
    split = Mesh(mesh.devices.reshape(4, 8, mesh.shape["col"]), ("row_0", "row_1", "col"))
    placed = (
        P(ROW, "col"),
        P("col", ROW),
        P(ROW, "col", None),
        P(ROW, "col", None),
        P(ROW, "col"),
        P("col", ROW),
    )
    return jax.shard_map(
        on_device,
        mesh=split,
        in_specs=placed,
        out_specs=(P("col", ROW), P(ROW, "col"), P("col", ROW)),
        check_vma=False,
    )
```

profile of v0, /device:TPU:1, one launch (start us, length us, event | category | flops | bytes accessed | tf_op | source)
XLA Modules:
  0.0 455.6 jit_solution(8898258210480005376)
XLA Ops:
  7.2 13.0 %all-gather = bf16[192,1024]{1,0:T(8,128)(2,1)} all-gather(bf16[48,1024]{1,0:T(8,128)(2,1)} %param.12), channel_id=2, replica_groups=mesh['row_0'=4,'row_1'=8,'col'=8] {'row_0'}, dimensions={0}, use_global_device_ids=true | all-gather | bytes 491520 | tf_op jit(solution)/shard_map/all_gather | solution.py:20
  24.8 44.5 %all-gather.7.cloned.1.call-done = bf16[32,48,1024]{2,1,0:T(8,128)(2,1)} async-done(((bf16[4,48,1024]{2,1,0:T(8,128)(2,1)}), bf16[32,48,1024]{2,1,0:T(8,128)(2,1)}) %all-gather.7.cloned.1.call-update) | async-done | bytes 3145744 | tf_op jit(solution)/shard_map/all_gather | solution.py:20
  69.2 4.1 copy.27
  73.3 3.5 broadcast.138.clone
  76.8 66.5 %while.33 = (s32[]{:T(128)}, f32[12,128,1024]{2,1,0:T(8,128)}, bf16[12,128,1024]{2,1,0:T(8,128)(2,1)}, bf16[32,128,128]{2,1,0:T(8,128)(2,1)S(1)}, s32[32]{0:T(128)S(1)}, /*index=5*/s32[32]{0:T(128)S(1)}, s32[]{:T(128)}) while((s32[]{:T(128)}, f32[12,128,1024]{2,1,0:T(8,128)}, bf16[12,128,1024]{2,1,0:T(8,128)(2,1)}, ...), condition=%wide.region_1.2_spmd.clone, body=%wide.region_0.1_spmd.clone.sunk | while | flops 193463296 | bytes 11273041 | solution.py:61
  79.0 2.4 fusion.79
  84.5 2.4 fusion.79
  95.6 2.4 fusion.79
  123.3 2.4 fusion.79
  143.4 43.4 %reduce-scatter.4.cloned.1.call-done = f32[192,1024]{1,0:T(8,128)} async-done(((f32[1536,1024]{1,0:T(8,128)}), f32[192,1024]{1,0:T(8,128)}) %reduce-scatter.4.cloned.1.call-update) | async-done | bytes 786448 | tf_op jit(solution)/shard_map/reduce_scatter | solution.py:104
  186.8 2.4 multiply_convert_fusion
  189.2 31.1 %all-gather.5.cloned.1.call-done = bf16[1536,1024]{1,0:T(8,128)(2,1)} async-done(((bf16[192,1024]{1,0:T(8,128)(2,1)}), bf16[1536,1024]{1,0:T(8,128)(2,1)}) %all-gather.5.cloned.1.call-update) | async-done | bytes 3145744 | tf_op jit(solution)/shard_map/all_gather | solution.py:114
  220.3 3.5 broadcast.138
  223.8 68.4 %while.34 = (s32[]{:T(128)}, f32[12,128,1024]{2,1,0:T(8,128)}, bf16[12,128,1024]{2,1,0:T(8,128)(2,1)}, bf16[32,128,128]{2,1,0:T(8,128)(2,1)S(1)}, s32[32]{0:T(128)S(1)}, /*index=5*/s32[32]{0:T(128)S(1)}, s32[]{:T(128)}) while((s32[]{:T(128)}, f32[12,128,1024]{2,1,0:T(8,128)}, bf16[12,128,1024]{2,1,0:T(8,128)(2,1)}, ...), condition=%wide.region_4.5_spmd.clone, body=%wide.region_3.4_spmd.clone.sunk | while | flops 193463296 | bytes 11273041 | solution.py:61
  294.1 2.6 copy.39
  296.7 2.5 copy.40
  299.1 59.5 %reduce-scatter.6.cloned.1.call-done = f32[384,1024]{1,0:T(8,128)} async-done(((f32[1536,1024]{1,0:T(8,128)}), f32[384,1024]{1,0:T(8,128)}) %reduce-scatter.6.cloned.1.call-update) | async-done | bytes 1572880 | tf_op jit(solution)/shard_map/reduce_scatter | solution.py:33
  358.6 72.4 %while.35 = (s32[]{:T(128)}, f32[32,128,128]{2,1,0:T(8,128)}, bf16[12,128,8,128]{3,2,1,0:T(8,128)(2,1)}, s32[32]{0:T(128)S(1)}, bf16[12,128,8,128]{3,2,1,0:T(8,1...) while((s32[]{:T(128)}, f32[32,128,128]{2,1,0:T(8,128)}, bf16[12,128,8,128]{3,2,1,0:T(8,128)(2,1)}, ...), condition=%wide.region_8.9_spmd.clone, body=%wide.region_7.8_spmd.clone.sunk | while | flops 135268544 | bytes 12592227 | solution.py:82
  365.9 3.4 select_add_fusion.2
  372.1 3.5 select_add_fusion.2
  378.3 3.5 select_add_fusion.2
  384.5 3.5 select_add_fusion.2
  390.6 3.5 select_add_fusion.2
  396.8 3.4 select_add_fusion.2
  403.0 3.4 select_add_fusion.2
  409.1 3.4 select_add_fusion.2
  415.3 3.4 select_add_fusion.2
  421.4 3.4 select_add_fusion.2
  427.6 3.4 select_add_fusion.2
  432.8 2.5 broadcast_in_dim.11
  435.3 6.3 %scatter_fusion = f32[64,128,128]{2,1,0:T(8,128)} fusion(f32[64,128,128]{2,1,0:T(8,128)} %broadcast_in_dim.11, s32[32]{0:T(128)S(1)} %get-tuple-element.217, f32[32,128,128]{2,1,0:T(8,128)S(1)} %broadcast_multiply_fusion), kind=kCustom, calls=%fused_computation.3 | custom fusion | flops 524288 | bytes 6291584 | tf_op jit(solution)/shard_map/scatter-add | solution.py:86
  441.6 2.6 convert_element_type.74
  (295 shorter events, 170.8 us)
Async XLA Ops:
  7.2 62.1 %all-gather.7.cloned.1.call-start = ((), (), s32[]{:S(2)}) async-start(), calls=%async_computation.7 | async-start | bytes 3538944 | tf_op jit(solution)/shard_map/all_gather | solution.py:20
  20.2 166.5 %reduce-scatter.4.cloned.1.call-start = ((), (), s32[]{:S(2)}) async-start(), calls=%async_computation.3 | async-start | bytes 7077888 | tf_op jit(solution)/shard_map/reduce_scatter | solution.py:104
  22.5 1.3 copy-start.3
  22.5 1.3 copy-start.4
  143.3 43.5 %copy-start.2 = (bf16[192,1024]{1,0:T(8,128)(2,1)S(1)}, bf16[192,1024]{1,0:T(8,128)(2,1)}, u32[]{:S(2)}) copy-start(bf16[192,1024]{1,0:T(8,128)(2,1)} %param.17) | copy-start | bytes 1179652
  143.3 77.0 %all-gather.5.cloned.1.call-start = ((), (), s32[]{:S(2)}) async-start(), calls=%async_computation.4 | async-start | bytes 3538944 | tf_op jit(solution)/shard_map/all_gather | solution.py:114
  189.2 169.4 %reduce-scatter.6.cloned.1.call-start = ((), (), s32[]{:S(2)}) async-start(), calls=%async_computation.5 | async-start | bytes 7864320 | tf_op jit(solution)/shard_map/reduce_scatter | solution.py:33
  292.2 1.9 copy-start
  292.2 155.3 %reduce-scatter.8.cloned.1.call-start = ((), (), s32[]{:S(2)}) async-start(), calls=%async_computation.6 | async-start | bytes 1769472 | tf_op jit(solution)/shard_map/reduce_scatter | solution.py:33
  294.1 2.6 copy-start.1
Sparse Core Ops, SparseCore 0:
  20.4 48.8 all-gather.6
  143.4 43.3 reduce-scatter.3
  189.3 30.9 all-gather.4
  292.4 66.2 reduce-scatter.5
  361.0 35.9 reduce-scatter.7
where the time goes:
time: 457 us; the launch traced here: 456 us
  waiting for transfers between devices  179 us (39%)
  matrix products  127 us (28%)
  local copies, waits for them, and re-layouts  105 us (23%)
  other arithmetic  14.9 us (3%)
  between operations  14.6 us (3%)
  blocking collectives  13 us (3%)
    reduce_scatter x2, waiting for transfers between devices, own_rows(): so_far = lax.psum_scatter(so_far, axis, scatter_dimension=0, tiled=True)  59.5 us
    dot_general x24, matrix products, per_block(): jnp.einsum('bkq,kc->bcq', product, placer, precision=lax.Precision.HIGHEST)  56.6 us
    all_gather x1, waiting for transfers between devices, all_blocks(): pieces = lax.all_gather(pieces, axes[k])  44.5 us
    reduce_scatter x1, waiting for transfers between devices, on_device(): lax.psum_scatter(sparse_apply(full_tokens, live_tiles, local_rows, local_...  43.4 us
    dot_general x12, matrix products, accumulate(): jnp.einsum('bkp,bkq->kpq', token_block[:, local_rows], grad_block[:, loca...  39.8 us
    all_gather x1, waiting for transfers between devices, on_device(): full_grads = lax.all_gather(grad_pre, 'col', axis=0, tiled=True)  31.1 us
    while x48, local copies, waits for them, and re-layouts  24.3 us
    dynamic_update_slice x24, local copies, waits for them, and re-layouts, sparse_apply(): return lax.map(per_block, stacked).reshape(count_rows, out_blocks * TILE)  20.5 us
  transfers between devices with their start and end apart: 5, of which 4 were waited for; matrix products, arithmetic and copies ran while one was open for 21% of the time, Pallas kernels for 0%

commit v1 on v0

--- a/solution.py
+++ b/solution.py
@@ -111,7 +111,12 @@
     hidden = (pre_act * gate_value).astype(jnp.bfloat16)
     silu_slope = gate_value * (1.0 + pre_act * (1.0 - gate_value))
     grad_pre = (hidden_cotangent.astype(jnp.float32) * silu_slope).astype(jnp.bfloat16)
-    full_grads = lax.all_gather(grad_pre, "col", axis=0, tiled=True)
+    ring = [grad_pre]
+    for hop in range(7):
+        ring.append(lax.ppermute(ring[-1], "col", [(dev, (dev + 1) % 8) for dev in range(8)]))
+    full_grads = jnp.roll(
+        jnp.concatenate(ring[::-1], axis=0), (lax.axis_index("col") + 1) * ring[0].shape[0], axis=0
+    )
     input_grad = own_rows(
         sparse_apply(full_grads, live_tiles, local_cols, local_rows, row_blocks, True), ROW
     ).astype(jnp.bfloat16)

time: 457 us -> 493 us (1.079)
  waiting for transfers between devices: 179 us -> 196 us
  starting transfers between devices: 0.39 us -> 9.85 us
  local copies, waits for them, and re-layouts: 105 us -> 113 us
    ppermute x0 -> x7, waiting for transfers between devices: none -> 44.1 us  [on_device(): lax.ppermute(ring[-1], 'col', [(dev, (dev + 1) % 8) for dev in range(8)])]
    all_gather x1 -> x0, waiting for transfers between devices: 31.1 us -> none  [on_device(): full_grads = lax.all_gather(grad_pre, 'col', axis=0, tiled=True)]
    ppermute x0 -> x7, starting transfers between devices: none -> 9.28 us  [on_device(): lax.ppermute(ring[-1], 'col', [(dev, (dev + 1) % 8) for dev in range(8)])]
    unnamed x14 -> x32, local copies, waits for them, and re-layouts: 10.8 us -> 16.1 us
  transfers between devices with their start and end apart: 5 -> 11, of which waited for: 4 -> 10; matrix products, arithmetic and copies ran while one was open for 21% -> 20% of each run, Pallas kernels for 0% -> 0%
where the time goes in v1:
time: 493 us; the launch traced here: 491 us
  waiting for transfers between devices  196 us (40%)
  matrix products  127 us (26%)
  local copies, waits for them, and re-layouts  113 us (23%)
  other arithmetic  14.8 us (3%)
  between operations  14.7 us (3%)
  blocking collectives  13 us (3%)
  starting transfers between devices  9.85 us (2%)
    reduce_scatter x2, waiting for transfers between devices, own_rows(): so_far = lax.psum_scatter(so_far, axis, scatter_dimension=0, tiled=True)  64.2 us
    dot_general x24, matrix products, per_block(): jnp.einsum('bkq,kc->bcq', product, placer, precision=lax.Precision.HIGHEST)  56.6 us
    all_gather x1, waiting for transfers between devices, all_blocks(): pieces = lax.all_gather(pieces, axes[k])  44.5 us
    ppermute x7, waiting for transfers between devices, on_device(): lax.ppermute(ring[-1], 'col', [(dev, (dev + 1) % 8) for dev in range(8)])  44.1 us
    reduce_scatter x1, waiting for transfers between devices, on_device(): lax.psum_scatter(sparse_apply(full_tokens, live_tiles, local_rows, local_...  43.2 us
    dot_general x12, matrix products, accumulate(): jnp.einsum('bkp,bkq->kpq', token_block[:, local_rows], grad_block[:, loca...  39.8 us
    while x48, local copies, waits for them, and re-layouts  24.3 us
    dynamic_update_slice x24, local copies, waits for them, and re-layouts, sparse_apply(): return lax.map(per_block, stacked).reshape(count_rows, out_blocks * TILE)  20.3 us
  transfers between devices with their start and end apart: 11, of which 10 were waited for; matrix products, arithmetic and copies ran while one was open for 20% of the time, Pallas kernels for 0%

profile of v1, /device:TPU:1, one launch (start us, length us, event | category | flops | bytes accessed | tf_op | source)
XLA Modules:
  0.0 490.6 jit_solution(17066835462938625140)
XLA Ops:
  7.2 13.0 %all-gather = bf16[192,1024]{1,0:T(8,128)(2,1)} all-gather(bf16[48,1024]{1,0:T(8,128)(2,1)} %param.12), channel_id=2, replica_groups=mesh['row_0'=4,'row_1'=8,'col'=8] {'row_0'}, dimensions={0}, use_global_device_ids=true | all-gather | bytes 491520 | tf_op jit(solution)/shard_map/all_gather | solution.py:20
  24.8 44.5 %all-gather.4.cloned.1.call-done = bf16[32,48,1024]{2,1,0:T(8,128)(2,1)} async-done(((bf16[4,48,1024]{2,1,0:T(8,128)(2,1)}), bf16[32,48,1024]{2,1,0:T(8,128)(2,1)}) %all-gather.4.cloned.1.call-update) | async-done | bytes 3145744 | tf_op jit(solution)/shard_map/all_gather | solution.py:20
  69.3 4.0 copy.26
  73.3 3.5 broadcast.138.clone
  76.7 66.3 %while.33 = (s32[]{:T(128)}, f32[12,128,1024]{2,1,0:T(8,128)}, bf16[12,128,1024]{2,1,0:T(8,128)(2,1)}, bf16[32,128,128]{2,1,0:T(8,128)(2,1)S(1)}, s32[32]{0:T(128)S(1)}, /*index=5*/s32[32]{0:T(128)S(1)}, s32[]{:T(128)}) while((s32[]{:T(128)}, f32[12,128,1024]{2,1,0:T(8,128)}, bf16[12,128,1024]{2,1,0:T(8,128)(2,1)}, ...), condition=%wide.region_1.2_spmd.clone, body=%wide.region_0.1_spmd.clone.sunk | while | flops 193463296 | bytes 11273041 | solution.py:61
  143.3 43.2 %reduce-scatter.4.cloned.1.call-done = f32[192,1024]{1,0:T(8,128)} async-done(((f32[1536,1024]{1,0:T(8,128)}), f32[192,1024]{1,0:T(8,128)}) %reduce-scatter.4.cloned.1.call-update) | async-done | bytes 786448 | tf_op jit(solution)/shard_map/reduce_scatter | solution.py:104
  189.1 4.7 collective-permute-done
  196.3 4.7 collective-permute-done.1
  203.5 4.7 collective-permute-done.2
  210.7 5.8 %collective-permute-done.3 = bf16[192,1024]{1,0:T(8,128)(2,1)S(1)} collective-permute-done((bf16[192,1024]{1,0:T(8,128)(2,1)S(1)}, bf16[192,1024]{1,0:T(8,128)(2,1)S(1)}, u32[]{:S(2)}, u32[]{:S(2)}) %collective-permute-start.3) | collective-permute-done | bytes 393248 | tf_op jit(solution)/shard_map/ppermute | solution.py:116
  217.9 7.0 %collective-permute-done.4 = bf16[192,1024]{1,0:T(8,128)(2,1)S(1)} collective-permute-done((bf16[192,1024]{1,0:T(8,128)(2,1)S(1)}, bf16[192,1024]{1,0:T(8,128)(2,1)S(1)}, u32[]{:S(2)}, u32[]{:S(2)}) %collective-permute-start.4) | collective-permute-done | bytes 393248 | tf_op jit(solution)/shard_map/ppermute | solution.py:116
  225.1 8.4 %collective-permute-done.5 = bf16[192,1024]{1,0:T(8,128)(2,1)} collective-permute-done((bf16[192,1024]{1,0:T(8,128)(2,1)S(1)}, bf16[192,1024]{1,0:T(8,128)(2,1)}, u32[]{:S(2)}, u32[]{:S(2)}) %collective-permute-start.5) | collective-permute-done | bytes 393248 | tf_op jit(solution)/shard_map/ppermute | solution.py:116
  233.4 8.7 %collective-permute-done.6 = bf16[192,1024]{1,0:T(8,128)(2,1)} collective-permute-done((bf16[192,1024]{1,0:T(8,128)(2,1)}, bf16[192,1024]{1,0:T(8,128)(2,1)}, u32[]{:S(2)}, u32[]{:S(2)}) %collective-permute-start.6) | collective-permute-done | bytes 393248 | tf_op jit(solution)/shard_map/ppermute | solution.py:116
  246.7 3.0 constant_dynamic-slice_fusion.2
  249.7 3.4 broadcast.138
  253.1 68.4 %while.34 = (s32[]{:T(128)}, f32[12,128,1024]{2,1,0:T(8,128)}, bf16[12,128,1024]{2,1,0:T(8,128)(2,1)}, bf16[32,128,128]{2,1,0:T(8,128)(2,1)S(1)}, s32[32]{0:T(128)S(1)}, /*index=5*/s32[32]{0:T(128)S(1)}, s32[]{:T(128)}) while((s32[]{:T(128)}, f32[12,128,1024]{2,1,0:T(8,128)}, bf16[12,128,1024]{2,1,0:T(8,128)(2,1)}, ...), condition=%wide.region_4.5_spmd.clone, body=%wide.region_3.4_spmd.clone.sunk | while | flops 193463296 | bytes 11273041 | solution.py:61
  323.4 2.5 copy.38
  329.4 64.2 %reduce-scatter.6.cloned.1.call-done = f32[384,1024]{1,0:T(8,128)} async-done(((f32[1536,1024]{1,0:T(8,128)}), f32[384,1024]{1,0:T(8,128)}) %reduce-scatter.6.cloned.1.call-update) | async-done | bytes 1572880 | tf_op jit(solution)/shard_map/reduce_scatter | solution.py:33
  393.7 72.4 %while.35 = (s32[]{:T(128)}, f32[32,128,128]{2,1,0:T(8,128)}, bf16[12,128,8,128]{3,2,1,0:T(8,128)(2,1)}, s32[32]{0:T(128)S(1)}, bf16[12,128,8,128]{3,2,1,0:T(8,1...) while((s32[]{:T(128)}, f32[32,128,128]{2,1,0:T(8,128)}, bf16[12,128,8,128]{3,2,1,0:T(8,128)(2,1)}, ...), condition=%wide.region_8.9_spmd.clone, body=%wide.region_7.8_spmd.clone.sunk | while | flops 135268544 | bytes 12592227 | solution.py:82
  401.0 3.4 select_add_fusion.2
  407.1 3.5 select_add_fusion.2
  413.3 3.5 select_add_fusion.2
  419.5 3.5 select_add_fusion.2
  425.7 3.5 select_add_fusion.2
  431.9 3.4 select_add_fusion.2
  438.0 3.4 select_add_fusion.2
  444.2 3.4 select_add_fusion.2
  450.3 3.4 select_add_fusion.2
  456.5 3.4 select_add_fusion.2
  462.7 3.4 select_add_fusion.2
  470.4 6.2 %scatter_fusion = f32[64,128,128]{2,1,0:T(8,128)} fusion(f32[64,128,128]{2,1,0:T(8,128)} %broadcast_in_dim.11, s32[32]{0:T(128)S(1)} %get-tuple-element.211, f32[32,128,128]{2,1,0:T(8,128)S(1)} %broadcast_multiply_fusion), kind=kCustom, calls=%fused_computation.3 | custom fusion | flops 524288 | bytes 6291584 | tf_op jit(solution)/shard_map/scatter-add | solution.py:86
  476.6 2.6 convert_element_type.74
  (326 shorter events, 202.1 us)
Async XLA Ops:
  7.2 16.6 %copy-start.4 = (s32[1,1,32]{2,1,0:T(1,128)S(1)}, s32[1,1,32]{2,1,0:T(1,128)}, u32[]{:S(2)}) copy-start(s32[1,1,32]{2,1,0:T(1,128)} %param.14) | copy-start | bytes 388
  7.2 16.6 %copy-start.5 = (s32[1,1,32]{2,1,0:T(1,128)S(1)}, s32[1,1,32]{2,1,0:T(1,128)}, u32[]{:S(2)}) copy-start(s32[1,1,32]{2,1,0:T(1,128)} %param.15) | copy-start | bytes 388
  7.2 62.1 %all-gather.4.cloned.1.call-start = ((), (), s32[]{:S(2)}) async-start(), calls=%async_computation.6 | async-start | bytes 3538944 | tf_op jit(solution)/shard_map/all_gather | solution.py:20
  20.3 166.3 %reduce-scatter.4.cloned.1.call-start = ((), (), s32[]{:S(2)}) async-start(), calls=%async_computation.3 | async-start | bytes 7077888 | tf_op jit(solution)/shard_map/reduce_scatter | solution.py:104
  143.1 43.5 %copy-start.3 = (bf16[192,1024]{1,0:T(8,128)(2,1)S(1)}, bf16[192,1024]{1,0:T(8,128)(2,1)}, u32[]{:S(2)}) copy-start(bf16[192,1024]{1,0:T(8,128)(2,1)} %param.17) | copy-start | bytes 1179652
  143.1 250.6 %reduce-scatter.6.cloned.1.call-start = ((), (), s32[]{:S(2)}) async-start(), calls=%async_computation.4 | async-start | bytes 7864320 | tf_op jit(solution)/shard_map/reduce_scatter | solution.py:33
  188.8 5.0 %collective-permute-start = (bf16[192,1024]{1,0:T(8,128)(2,1)S(1)}, bf16[192,1024]{1,0:T(8,128)(2,1)S(1)}, u32[]{:S(2)}, u32[]{:S(2)}) collective-permute-start(bf16[192,1024]{1,0:T(8,128)(2,1)S(1)} %get-tuple-element.209), channel_id=1, source_target_pairs={{0,1},{1,2},{2,3},{3,4},{4,5},{5,6},{6,7},{7,0},{8,9},{9,10},{10,1... | collective-permute-start | bytes 1179656 | tf_op jit(solution)/shard_map/ppermute | solution.py:116
  193.8 7.2 %collective-permute-start.1 = (bf16[192,1024]{1,0:T(8,128)(2,1)S(1)}, bf16[192,1024]{1,0:T(8,128)(2,1)S(1)}, u32[]{:S(2)}, u32[]{:S(2)}) collective-permute-start(bf16[192,1024]{1,0:T(8,128)(2,1)S(1)} %collective-permute-done), channel_id=1, source_target_pairs={{0,1},{1,2},{2,3},{3,4},{4,5},{5,6},{6,7},{7,0},{8,9},{9,10},{10,1... | collective-permute-start | bytes 1179656 | tf_op jit(solution)/shard_map/ppermute | solution.py:116
  201.0 7.2 %collective-permute-start.2 = (bf16[192,1024]{1,0:T(8,128)(2,1)S(1)}, bf16[192,1024]{1,0:T(8,128)(2,1)S(1)}, u32[]{:S(2)}, u32[]{:S(2)}) collective-permute-start(bf16[192,1024]{1,0:T(8,128)(2,1)S(1)} %collective-permute-done.1), channel_id=1, source_target_pairs={{0,1},{1,2},{2,3},{3,4},{4,5},{5,6},{6,7},{7,0},{8,9},{9,10},{10,1... | collective-permute-start | bytes 1179656 | tf_op jit(solution)/shard_map/ppermute | solution.py:116
  208.2 8.3 %collective-permute-start.3 = (bf16[192,1024]{1,0:T(8,128)(2,1)S(1)}, bf16[192,1024]{1,0:T(8,128)(2,1)S(1)}, u32[]{:S(2)}, u32[]{:S(2)}) collective-permute-start(bf16[192,1024]{1,0:T(8,128)(2,1)S(1)} %collective-permute-done.2), channel_id=1, source_target_pairs={{0,1},{1,2},{2,3},{3,4},{4,5},{5,6},{6,7},{7,0},{8,9},{9,10},{10,1... | collective-permute-start | bytes 1179656 | tf_op jit(solution)/shard_map/ppermute | solution.py:116
  216.5 8.4 %collective-permute-start.4 = (bf16[192,1024]{1,0:T(8,128)(2,1)S(1)}, bf16[192,1024]{1,0:T(8,128)(2,1)S(1)}, u32[]{:S(2)}, u32[]{:S(2)}) collective-permute-start(bf16[192,1024]{1,0:T(8,128)(2,1)S(1)} %collective-permute-done.3), channel_id=1, source_target_pairs={{0,1},{1,2},{2,3},{3,4},{4,5},{5,6},{6,7},{7,0},{8,9},{9,10},{10,1... | collective-permute-start | bytes 1179656 | tf_op jit(solution)/shard_map/ppermute | solution.py:116
  224.9 8.5 %collective-permute-start.5 = (bf16[192,1024]{1,0:T(8,128)(2,1)S(1)}, bf16[192,1024]{1,0:T(8,128)(2,1)}, u32[]{:S(2)}, u32[]{:S(2)}) collective-permute-start(bf16[192,1024]{1,0:T(8,128)(2,1)S(1)} %collective-permute-done.4), channel_id=1, source_target_pairs={{0,1},{1,2},{2,3},{3,4},{4,5},{5,6},{6,7},{7,0},{8,9},{9,10},{10,1... | collective-permute-start | bytes 1179656 | tf_op jit(solution)/shard_map/ppermute | solution.py:116
  233.4 8.7 %collective-permute-start.6 = (bf16[192,1024]{1,0:T(8,128)(2,1)}, bf16[192,1024]{1,0:T(8,128)(2,1)}, u32[]{:S(2)}, u32[]{:S(2)}) collective-permute-start(bf16[192,1024]{1,0:T(8,128)(2,1)} %collective-permute-done.5), channel_id=1, source_target_pairs={{0,1},{1,2},{2,3},{3,4},{4,5},{5,6},{6,7},{7,0},{8,9},{9,10},{10,1... | collective-permute-start | bytes 1179656 | tf_op jit(solution)/shard_map/ppermute | solution.py:116
  246.7 6.4 %copy-start.1 = (bf16[3072,1024]{1,0:T(8,128)(2,1)}, bf16[3072,1024]{1,0:T(8,128)(2,1)S(1)}, u32[]{:S(2)}) copy-start(bf16[3072,1024]{1,0:T(8,128)(2,1)S(1)} %constant_dynamic-update-slice_fusion.2) | copy-start | bytes 18874372
  321.5 1.9 copy-start
  321.6 160.9 %reduce-scatter.8.cloned.1.call-start = ((), (), s32[]{:S(2)}) async-start(), calls=%async_computation.5 | async-start | bytes 1769472 | tf_op jit(solution)/shard_map/reduce_scatter | solution.py:33
  321.8 4.1 copy-start.2
Sparse Core Ops, SparseCore 0:
  20.4 48.8 all-gather.3
  143.2 43.3 reduce-scatter.3
  321.7 71.9 reduce-scatter.5
  396.1 36.0 reduce-scatter.7
